TPU v7x, 256 devices: a whole 4x4x8 slice. The times are simulated.
256 devices in a mesh: grp: 4 (over y), dev: 64 (over x, z, core).
Axes of the slice: x: 4, y: 4, z: 8, core: 2. Of those that a mesh axis runs over, the one named last changes fastest.
Arguments:
- field: float32 [512, 512, 256, 4], P('dev', 'grp'), may hold values from -21 to 21
- start_basis: float32 [512, 64], replicated, may hold values from -6 to 6
Outputs:
- factor: float32 [512, 64], replicated
- core: float32 [64, 512, 256, 4], P(None, ('grp', 'dev'))
All inputs are finite; a program needn't handle non-finite values.
Results may differ from a plain program's by a relative error of at most 0.0003.
Values sent between devices are 32-bit elements; how exact they have to be, the bound alone decides.
No kernel may reach another device: no remote copies, remote signals or barrier semaphores. Data moves between devices by JAX's collectives and lax.ppermute only.
A program may use at most 192 MiB of HBM per device.

v0:
```python
import jax
import jax.numpy as jnp
from jax import lax
from jax.sharding import PartitionSpec as P

ITERS = 3


def product(left, right):
    return jnp.dot(left, right, precision=lax.Precision.HIGHEST, preferred_element_type=jnp.float32)


def on_device(field, start_basis):
    regrouped = lax.all_to_all(field, "dev", split_axis=1, concat_axis=0, tiled=True)
    rows = regrouped.shape[0]
    local_cols = regrouped.shape[1] * regrouped.shape[2] * regrouped.shape[3]
    unfold = regrouped.reshape(rows, local_cols)
    local_gram = product(unfold, unfold.T)
    gram = lax.psum(local_gram, ("grp", "dev"))
    basis = start_basis
    for step in range(ITERS):
        image = product(gram, basis)
        cross = product(image.T, image)
        chol = jnp.linalg.cholesky(cross)
        basis = lax.linalg.triangular_solve(
            chol, image, left_side=False, lower=True, transpose_a=True
        )
    core = product(basis.T, unfold)
    return (
        basis,
        core.reshape(basis.shape[1], regrouped.shape[1], regrouped.shape[2], regrouped.shape[3]),
    )


def solution(mesh):
    placed = (P("dev", "grp", None, None), P())
    return jax.shard_map(
        on_device,
        mesh=mesh,
        in_specs=placed,
        out_specs=(P(), P(None, ("grp", "dev"), None, None)),
        check_vma=False,
    )
```

profile of v0, /device:TPU:2, one launch (start us, length us, event | category | flops | bytes accessed | tf_op | source)
XLA Modules:
  0.0 543.9 jit_solution(3584140676412488919)
XLA Ops:
  7.2 3.4 copy.14
  10.7 106.2 %all_to_all.15 = f32[8,128,256,4]{2,3,0,1:T(4,128)} all-to-all(f32[8,128,256,4]{2,3,0,1:T(4,128)S(1)} %copy.14), channel_id=1, replica_groups=mesh['grp'=4,'dev'=64] {'dev'}, dimensions={1} | all-to-all | bytes 8388608 | tf_op jit(solution)/shard_map/all_to_all | solution.py:14
  116.9 50.4 %copy.15 = f32[8,64,2,256,4]{0,1,4,3,2:T(8,128)} copy(f32[8,64,2,256,4]{3,4,0,2,1:T(4,128)} %bitcast.63) | data formatting | bytes 8388608 | tf_op jit(solution)/shard_map/all_to_all | solution.py:14
  167.2 48.3 %reshape.21 = f32[512,2048]{0,1:T(8,128)} reshape(f32[64,8,2,256,4]{1,0,4,3,2:T(8,128)} %bitcast.1) | data formatting | bytes 8388608 | tf_op jit(solution)/shard_map/reshape | solution.py:17
  215.5 11.3 %fusion.17 = f32[512,512]{1,0:T(8,128)} fusion(f32[512,2048]{0,1:T(8,128)} %reshape.21), kind=kOutput, calls=%fused_computation.31 | convolution fusion | flops 6442450944 | bytes 5242880 | tf_op jit(solution)/shard_map/dot_general | solution.py:10
  226.9 5.2 dot_general.36
  232.1 252.3 %all-reduce.2.cloned.1.call-done = f32[512,512]{1,0:T(8,128)} async-done(((f32[512,512]{1,0:T(8,128)}), f32[512,512]{1,0:T(8,128)}) %all-reduce.2.cloned.1.call-update) | async-done | bytes 1048592 | tf_op jit(solution)/shard_map/psum | solution.py:19
  484.4 2.4 fusion.18
  486.9 0.3 fusion.19
  487.2 0.1 copy.16
  487.2 5.8 %cholesky.59 = f32[64,64]{1,0:T(8,128)S(1)} custom-call(f32[64,64]{1,0:T(8,128)S(1)} %fusion.12), custom_call_target="Cholesky" | custom-call | tf_op jit(solution)/shard_map/jit(cholesky)/cholesky | solution.py:24
  493.1 0.6 compare_reduce_fusion.2
  493.8 0.7 fusion.3
  494.4 4.9 custom-call.7
  499.3 0.3 convolution_bitcast_fusion.1
  499.7 2.4 fusion.20
  502.0 0.3 fusion.21
  502.3 0.1 copy.17
  502.4 5.8 %cholesky.70 = f32[64,64]{1,0:T(8,128)S(1)} custom-call(f32[64,64]{1,0:T(8,128)S(1)} %fusion.10), custom_call_target="Cholesky" | custom-call | tf_op jit(solution)/shard_map/jit(cholesky)/cholesky | solution.py:24
  508.3 0.6 compare_reduce_fusion.1
  508.9 0.7 fusion.4
  509.6 4.9 custom-call.8
  514.5 0.3 convolution_bitcast_fusion
  514.8 1.1 fusion.22
  516.0 0.3 fusion.23
  516.3 5.8 %cholesky.81 = f32[64,64]{1,0:T(8,128)S(1)} custom-call(f32[64,64]{1,0:T(8,128)S(1)} %fusion.8), custom_call_target="Cholesky" | custom-call | tf_op jit(solution)/shard_map/jit(cholesky)/cholesky | solution.py:24
  522.2 0.6 compare_reduce_fusion
  522.9 0.7 fusion.5
  523.5 4.9 custom-call.9
  528.4 0.3 fusion.6
  528.8 7.1 %fusion = f32[64,2,256,4]{2,0,3,1:T(8,128)S(1)} fusion(f32[2,256,4,512]{3,2,1,0:T(4,128)} %dot_general.36, f32[64,512]{1,0:T(8,128)S(1)} %fusion.6), kind=kOutput, calls=%fused_computation | convolution fusion | flops 805306368 | bytes 4849664 | tf_op jit(solution)/shard_map/dot_general | solution.py:10
  535.9 1.1 copy.20
  (15 shorter events, 0.3 us)
Async XLA Ops:
  7.2 477.3 %copy-start = (f32[512,64]{0,1:T(8,128)S(1)}, f32[512,64]{0,1:T(8,128)}, u32[]{:S(2)}) copy-start(f32[512,64]{0,1:T(8,128)} %param.6) | copy-start | bytes 393220
  7.2 477.3 %all-reduce.2.cloned.1.call-start = ((), (), s32[]{:S(2)}) async-start(), calls=%async_computation.1 | async-start | bytes 2097152 | tf_op jit(solution)/shard_map/psum | solution.py:19
  484.4 30.4 %copy-start.1 = (f32[512,512]{1,0:T(8,128)S(1)}, f32[512,512]{1,0:T(8,128)}, u32[]{:S(2)}) copy-start(f32[512,512]{1,0:T(8,128)} %all-reduce.2.cloned.1.call-done) | copy-start | bytes 3145732
  528.8 8.3 %copy-start.2 = (f32[64,512]{1,0:T(8,128)}, f32[64,512]{1,0:T(8,128)S(1)}, u32[]{:S(2)}) copy-start(f32[64,512]{1,0:T(8,128)S(1)} %fusion.6) | copy-start | bytes 393220
Sparse Core Ops, SparseCore 0:
  227.0 257.3 all-reduce.1
where the time goes:
time: 545 us; the launch traced here: 544 us
  waiting for transfers between devices  252 us (46%)
  local copies, waits for them, and re-layouts  109 us (20%)
  blocking collectives  106 us (19%)
  other arithmetic  36.2 us (7%)
  matrix products  26.2 us (5%)
  between operations  14.2 us (3%)
    psum x1, waiting for transfers between devices, on_device(): gram = lax.psum(local_gram, ('grp', 'dev'))  252 us
    all_to_all x1, blocking collectives, on_device(): lax.all_to_all(field, 'dev', split_axis=1, concat_axis=0, tiled=True)  106 us
    all_to_all x1, local copies, waits for them, and re-layouts, on_device(): lax.all_to_all(field, 'dev', split_axis=1, concat_axis=0, tiled=True)  50.4 us
    reshape x1, local copies, waits for them, and re-layouts, on_device(): unfold = regrouped.reshape(rows, local_cols)  48.3 us
    dot_general x8, matrix products, product(): jnp.dot(left, right, precision=lax.Precision.HIGHEST, preferred_element_t...  25.2 us
    another operation x9, other arithmetic, on_device(): chol = jnp.linalg.cholesky(cross)  19.6 us
    another operation x6, other arithmetic, on_device(): lax.linalg.triangular_solve(chol, image, left_side=False, lower=True, tra...  16.6 us
  transfers between devices with their start and end apart: 1, of which 1 were waited for; matrix products, arithmetic and copies ran while one was open for 1% of the time, Pallas kernels for 0%

commit v1 on v0

--- a/solution.py
+++ b/solution.py
@@ -16,7 +16,11 @@
     local_cols = regrouped.shape[1] * regrouped.shape[2] * regrouped.shape[3]
     unfold = regrouped.reshape(rows, local_cols)
     local_gram = product(unfold, unfold.T)
-    gram = lax.psum(local_gram, ("grp", "dev"))
+
+    def arrange_core(incoming_x):
+        return lax.psum(lax.psum(incoming_x, axis_name="dev"), axis_name="grp")
+
+    gram = arrange_core(local_gram)
     basis = start_basis
     for step in range(ITERS):
         image = product(gram, basis)

time: 545 us -> 524 us (0.961)
  waiting for transfers between devices: 252 us -> 231 us
    psum x1 -> x2, waiting for transfers between devices: 252 us -> 231 us  [arrange_core(): return lax.psum(lax.psum(incoming_x, axis_name='dev'), axis_name='grp')]
  transfers between devices with their start and end apart: 1 -> 2, of which waited for: 1 -> 2; matrix products, arithmetic and copies ran while one was open for 1% -> 1% of each run, Pallas kernels for 0% -> 0%
where the time goes in v1:
time: 524 us; the launch traced here: 523 us
  waiting for transfers between devices  231 us (44%)
  local copies, waits for them, and re-layouts  109 us (21%)
  blocking collectives  106 us (20%)
  other arithmetic  36.2 us (7%)
  matrix products  26.1 us (5%)
  between operations  14.2 us (3%)
    psum x2, waiting for transfers between devices, arrange_core(): return lax.psum(lax.psum(incoming_x, axis_name='dev'), axis_name='grp')  231 us
    all_to_all x1, blocking collectives, on_device(): lax.all_to_all(field, 'dev', split_axis=1, concat_axis=0, tiled=True)  106 us
    all_to_all x1, local copies, waits for them, and re-layouts, on_device(): lax.all_to_all(field, 'dev', split_axis=1, concat_axis=0, tiled=True)  50.4 us
    reshape x1, local copies, waits for them, and re-layouts, on_device(): unfold = regrouped.reshape(rows, local_cols)  48.3 us
    dot_general x8, matrix products, product(): jnp.dot(left, right, precision=lax.Precision.HIGHEST, preferred_element_t...  25.1 us
    another operation x9, other arithmetic, on_device(): chol = jnp.linalg.cholesky(cross)  19.6 us
    another operation x6, other arithmetic, on_device(): lax.linalg.triangular_solve(chol, image, left_side=False, lower=True, tra...  16.6 us
  transfers between devices with their start and end apart: 2, of which 2 were waited for; matrix products, arithmetic and copies ran while one was open for 1% of the time, Pallas kernels for 0%

profile of v1, /device:TPU:2, one launch (start us, length us, event | category | flops | bytes accessed | tf_op | source)
XLA Modules:
  0.0 523.0 jit_solution(11063321987038324154)
XLA Ops:
  7.2 3.4 copy.14
  10.7 106.2 %all_to_all.15 = f32[8,128,256,4]{2,3,0,1:T(4,128)} all-to-all(f32[8,128,256,4]{2,3,0,1:T(4,128)S(1)} %copy.14), channel_id=1, replica_groups=mesh['grp'=4,'dev'=64] {'dev'}, dimensions={1} | all-to-all | bytes 8388608 | tf_op jit(solution)/shard_map/all_to_all | solution.py:14
  116.9 50.4 %copy.15 = f32[8,64,2,256,4]{0,1,4,3,2:T(8,128)} copy(f32[8,64,2,256,4]{3,4,0,2,1:T(4,128)} %bitcast.63) | data formatting | bytes 8388608 | tf_op jit(solution)/shard_map/all_to_all | solution.py:14
  167.2 48.3 %reshape.21 = f32[512,2048]{0,1:T(8,128)} reshape(f32[64,8,2,256,4]{1,0,4,3,2:T(8,128)} %bitcast.1) | data formatting | bytes 8388608 | tf_op jit(solution)/shard_map/reshape | solution.py:17
  215.5 11.3 %fusion.17 = f32[512,512]{1,0:T(8,128)} fusion(f32[512,2048]{0,1:T(8,128)} %reshape.21), kind=kOutput, calls=%fused_computation.31 | convolution fusion | flops 6442450944 | bytes 5242880 | tf_op jit(solution)/shard_map/dot_general | solution.py:10
  226.9 185.8 %all-reduce.3.cloned.1.call-done = f32[512,512]{1,0:T(8,128)} async-done(((f32[512,512]{1,0:T(8,128)}), f32[512,512]{1,0:T(8,128)}) %all-reduce.3.cloned.1.call-update) | async-done | bytes 1048592 | tf_op jit(solution)/shard_map/psum | solution.py:21
  412.8 5.2 dot_general.36
  418.0 45.6 %all-reduce.5.cloned.1.call-done = f32[512,512]{1,0:T(8,128)} async-done(((f32[512,512]{1,0:T(8,128)}), f32[512,512]{1,0:T(8,128)}) %all-reduce.5.cloned.1.call-update) | async-done | bytes 1048592 | tf_op jit(solution)/shard_map/psum | solution.py:21
  463.6 2.4 fusion.18
  466.0 0.3 fusion.19
  466.3 0.1 copy.16
  466.4 5.8 %cholesky.59 = f32[64,64]{1,0:T(8,128)S(1)} custom-call(f32[64,64]{1,0:T(8,128)S(1)} %fusion.12), custom_call_target="Cholesky" | custom-call | tf_op jit(solution)/shard_map/jit(cholesky)/cholesky | solution.py:28
  472.3 0.6 compare_reduce_fusion.2
  472.9 0.7 fusion.3
  473.6 4.9 custom-call.7
  478.5 0.3 convolution_bitcast_fusion.1
  478.8 2.4 fusion.20
  481.2 0.3 fusion.21
  481.6 5.8 %cholesky.70 = f32[64,64]{1,0:T(8,128)S(1)} custom-call(f32[64,64]{1,0:T(8,128)S(1)} %fusion.10), custom_call_target="Cholesky" | custom-call | tf_op jit(solution)/shard_map/jit(cholesky)/cholesky | solution.py:28
  487.4 0.6 compare_reduce_fusion.1
  488.1 0.7 fusion.4
  488.7 4.9 custom-call.8
  493.6 0.3 convolution_bitcast_fusion
  494.0 1.1 fusion.22
  495.1 0.3 fusion.23
  495.5 5.8 %cholesky.81 = f32[64,64]{1,0:T(8,128)S(1)} custom-call(f32[64,64]{1,0:T(8,128)S(1)} %fusion.8), custom_call_target="Cholesky" | custom-call | tf_op jit(solution)/shard_map/jit(cholesky)/cholesky | solution.py:28
  501.4 0.6 compare_reduce_fusion
  502.0 0.7 fusion.5
  502.7 4.9 custom-call.9
  507.6 0.3 fusion.6
  507.9 7.1 %fusion = f32[64,2,256,4]{2,0,3,1:T(8,128)S(1)} fusion(f32[2,256,4,512]{3,2,1,0:T(4,128)} %dot_general.36, f32[64,512]{1,0:T(8,128)S(1)} %fusion.6), kind=kOutput, calls=%fused_computation | convolution fusion | flops 805306368 | bytes 4849664 | tf_op jit(solution)/shard_map/dot_general | solution.py:10
  515.0 1.1 copy.20
  (18 shorter events, 0.4 us)
Async XLA Ops:
  7.2 456.4 %copy-start = (f32[512,64]{0,1:T(8,128)S(1)}, f32[512,64]{0,1:T(8,128)}, u32[]{:S(2)}) copy-start(f32[512,64]{0,1:T(8,128)} %param.6) | copy-start | bytes 393220
  7.2 405.6 %all-reduce.3.cloned.1.call-start = ((), (), s32[]{:S(2)}) async-start(), calls=%async_computation.1 | async-start | bytes 2097152 | tf_op jit(solution)/shard_map/psum | solution.py:21
  226.9 236.7 %all-reduce.5.cloned.1.call-start = ((), (), s32[]{:S(2)}) async-start(), calls=%async_computation.2 | async-start | bytes 2097152 | tf_op jit(solution)/shard_map/psum | solution.py:21
  463.6 30.4 %copy-start.1 = (f32[512,512]{1,0:T(8,128)S(1)}, f32[512,512]{1,0:T(8,128)}, u32[]{:S(2)}) copy-start(f32[512,512]{1,0:T(8,128)} %all-reduce.5.cloned.1.call-done) | copy-start | bytes 3145732
  507.9 8.3 %copy-start.2 = (f32[64,512]{1,0:T(8,128)}, f32[64,512]{1,0:T(8,128)S(1)}, u32[]{:S(2)}) copy-start(f32[64,512]{1,0:T(8,128)S(1)} %fusion.6) | copy-start | bytes 393220
Sparse Core Ops, SparseCore 0:
  227.0 185.7 all-reduce.2
  415.1 48.4 all-reduce.4
